TPU v7x, 32 devices: a whole 2x2x4 slice. The times are simulated.
32 devices in a mesh: section: 8 (over z, x), dp: 4 (over y, core).
Axes of the slice: x: 2, y: 2, z: 4, core: 2. Of those that a mesh axis runs over, the one named last changes fastest.
Arguments:
- act_in: bfloat16 [8, 128, 2048], P('section', None, 'dp'), may hold values from -6 to 6
- saved_act: bfloat16 [8, 128, 2048], P('section', None, 'dp'), may hold values from -6 to 6
- cotangent: bfloat16 [8, 128, 2048], P('section', None, 'dp'), may hold values from -6 to 6
- weight_xz: bfloat16 [8, 2048, 8192], P('section', 'dp'), may hold values from -0.125 to 0.125
- weight_bcdt: bfloat16 [8, 320, 2048], P('section', None, 'dp'), may hold values from -0.125 to 0.125
- weight_out: bfloat16 [8, 4096, 2048], P('section', None, 'dp'), may hold values from -0.09375 to 0.09375
- conv_x: float32 [8, 4, 4096], P('section', None, 'dp'), may hold values from -3 to 3
- conv_bc: float32 [8, 4, 256], P('section'), may hold values from -3 to 3
- dt_bias: float32 [8, 64], P('section', 'dp'), may hold values from -8 to -2
- a_log: float32 [8, 64], P('section', 'dp'), may hold values from 0 to 2.7
- d_skip: float32 [8, 64], P('section', 'dp'), may hold values from 0.5 to 1.5
- norm_gain: float32 [8, 4096], P('section', 'dp'), may hold values from 0.1 to 1.9
Outputs:
- next_act: bfloat16 [8, 128, 2048], P('section', None, 'dp')
- prev_grad: bfloat16 [8, 128, 2048], P('section', None, 'dp')
- grad_xz: float32 [8, 2048, 8192], P('section', 'dp')
- grad_bcdt: float32 [8, 320, 2048], P('section', None, 'dp')
- grad_out: float32 [8, 4096, 2048], P('section', None, 'dp')
All inputs are finite; a program needn't handle non-finite values.
Results may differ from a plain program's by a relative error of at most 0.0084.
Values may be sent and summed in bfloat16 or wider, within the bound.
A program may use at most 128 MiB of HBM per device.

v0:
```python
import jax
import jax.numpy as jnp
from jax import lax
from jax.sharding import PartitionSpec as P

D = 2048
HEAD_DIM = 64
NSTATE = 128
HEADS = 64
SEQ = 128
INNER = 4096


def from_behind(x, axis, by):
    length = lax.axis_size(axis)
    return lax.ppermute(x, axis, [(i, (i + by) % length) for i in range(length)])


def causal_conv(values, kernel_taps):
    kernel = kernel_taps.shape[0]
    length = values.shape[1]
    padded = jnp.pad(values, ((0, 0), (kernel - 1, 0), (0, 0)))
    running = jnp.zeros_like(values)
    for offset in range(kernel):
        running = running + kernel_taps[offset] * padded[:, offset : offset + length]
    return running


def map_scores(maps):
    input_map = maps[:, :, :NSTATE]
    output_map = maps[:, :, NSTATE:]
    return lax.dot_general(
        output_map, input_map, (((2,), (2,)), ((0,), (0,))), preferred_element_type=jnp.float32
    )


def map_grads(d_scores, maps):
    values = maps.astype(jnp.float32)
    input_map = values[:, :, :NSTATE]
    output_map = values[:, :, NSTATE:]
    d_input = jnp.einsum("bts,btn->bsn", d_scores, output_map, precision=lax.Precision.HIGHEST)
    d_output = jnp.einsum("bts,bsn->btn", d_scores, input_map, precision=lax.Precision.HIGHEST)
    return jnp.concatenate([d_input, d_output], axis=2)


def mixer(proj_x, proj_z, proj_dt, scores, conv_taps, dt_offset, log_rate, skip_gain):
    batch, length, width = proj_x.shape
    nheads = dt_offset.shape[0]
    head_width = width // nheads
    xconv = jax.nn.silu(causal_conv(proj_x, conv_taps))
    steps = jax.nn.softplus(proj_dt + dt_offset)
    cumul = jnp.cumsum(steps * -jnp.exp(log_rate), axis=1)
    position = jnp.arange(length)
    causal = (position[:, None] >= position[None, :])[None, None]
    heads_cum = jnp.swapaxes(cumul, 1, 2)
    spread = heads_cum[:, :, :, None] - heads_cum[:, :, None, :]
    decay = jnp.where(causal, jnp.exp(jnp.where(causal, spread, 0.0)), 0.0)
    weights = decay * scores[:, None] * jnp.swapaxes(steps, 1, 2)[:, :, None, :]
    heads_in = xconv.reshape(batch, length, nheads, head_width)
    result = jnp.einsum("bhts,bshp->bthp", weights, heads_in, precision=lax.Precision.HIGHEST)
    result = result + skip_gain[None, None, :, None] * heads_in
    gate_in = jax.nn.silu(proj_z.reshape(batch, length, nheads, head_width))
    return (result * gate_in).reshape(batch * length, width)


def times_transposed(left, right):
    return lax.dot_general(
        left, right, (((1,), (1,)), ((), ())), preferred_element_type=jnp.float32
    )


def transposed_times(left, right):
    return lax.dot_general(
        left, right, (((0,), (0,)), ((), ())), preferred_element_type=jnp.float32
    )


def feature_sum(values):
    return lax.psum(jnp.sum(values, axis=1), "dp")


def gate_sum(values):
    return lax.psum(jnp.sum(values, axis=1), "dp")


def send_along(row_block, direction):
    return from_behind(row_block, "section", direction)


def per_device(
    act_in,
    saved_act,
    cotangent,
    weight_xz,
    weight_bcdt,
    weight_out,
    conv_x,
    conv_bc,
    dt_bias,
    a_log,
    d_skip,
    norm_gain,
):
    input_rows = act_in[0]
    saved_rows = saved_act[0]
    cot_rows = cotangent[0]
    local_xz = weight_xz[0]
    local_bcdt = weight_bcdt[0]
    local_out = weight_out[0]
    taps_x = conv_x[0]
    taps_bc = conv_bc[0]
    dt_offset = dt_bias[0]
    log_rate = a_log[0]
    skip_gain = d_skip[0]
    gain_local = norm_gain[0]
    own_heads = dt_offset.shape[0]
    head_first = lax.axis_index("dp") * own_heads
    map_cols = 2 * NSTATE

    def whole_act(pre_part):
        batches = pre_part.shape[0] // SEQ
        conv_in = pre_part.reshape(batches, SEQ, map_cols)
        return jax.nn.silu(causal_conv(conv_in, taps_bc)).reshape(pre_part.shape)

    def project(rows):
        values = rows.astype(jnp.float32)
        scales = lax.rsqrt(feature_sum(values * values)[:, None] / D + 1e-05)
        normed = (values * scales).astype(jnp.bfloat16)
        part_xz = jnp.dot(normed, local_xz, preferred_element_type=jnp.float32)
        part_bcdt = times_transposed(normed, local_bcdt)
        own_xz = lax.psum_scatter(part_xz, "dp", scatter_dimension=1, tiled=True)
        whole_cols = lax.psum(part_bcdt, "dp")
        pre_part = whole_cols[:, :map_cols]
        maps = whole_act(pre_part).astype(jnp.bfloat16)
        own_dt = lax.dynamic_slice_in_dim(whole_cols[:, map_cols:], head_first, own_heads, 1)
        return (values, normed, scales, own_xz, pre_part, maps, own_dt)

    def gate_parts(projected):
        own_xz = projected[3]
        maps = projected[5]
        own_dt = projected[6]
        batches = own_xz.shape[0] // SEQ
        width = own_heads * HEAD_DIM
        split_xz = own_xz.reshape(batches, SEQ, own_heads, 2, HEAD_DIM)
        mix_x = split_xz[:, :, :, 0].reshape(batches, SEQ, width)
        mix_z = split_xz[:, :, :, 1].reshape(batches, SEQ, width)
        maps_three = maps.reshape(batches, SEQ, map_cols)
        scores = map_scores(maps_three)

        def local_mix(in_x, in_z, in_dt, in_scores):
            return mixer(in_x, in_z, in_dt, in_scores, taps_x, dt_offset, log_rate, skip_gain)

        gated, mix_back = jax.vjp(
            local_mix, mix_x, mix_z, own_dt.reshape(batches, SEQ, own_heads), scores
        )
        inverse = lax.rsqrt(gate_sum(gated * gated)[:, None] / INNER + 1e-05)
        mixed_in = (gated * inverse * gain_local).astype(jnp.bfloat16)
        return (gated, mix_back, inverse, mixed_in, maps_three)

    forward_proj = project(input_rows)
    back_proj = project(saved_rows)
    forward_mixed = gate_parts(forward_proj)[3]
    mixed = jnp.dot(
        lax.all_gather(forward_mixed, "dp", axis=1, tiled=True),
        local_out,
        preferred_element_type=jnp.float32,
    )
    section_out = (input_rows.astype(jnp.float32) + mixed).astype(jnp.bfloat16)
    next_act = send_along(section_out, 1)
    values, normed, scales, own_xz, pre_part, maps, own_dt = back_proj
    gated, mix_back, inverse, mixed_in, maps_three = gate_parts(back_proj)
    row_count = values.shape[0]
    grad_out = transposed_times(lax.all_gather(mixed_in, "dp", axis=1, tiled=True), cot_rows)
    d_mixed = lax.psum_scatter(
        times_transposed(cot_rows, local_out), "dp", scatter_dimension=1, tiled=True
    )
    dots = gate_sum(d_mixed * gain_local * gated)
    d_gated = (
        inverse * gain_local * d_mixed
        - gated * (inverse * inverse * inverse) * dots[:, None] / INNER
    )
    d_px, d_pz, d_pdt, d_scores = mix_back(d_gated)
    d_maps = map_grads(d_scores, maps_three).reshape(row_count, map_cols)
    d_dt_full = lax.dynamic_update_slice_in_dim(
        jnp.zeros((row_count, HEADS), jnp.float32),
        d_pdt.reshape(row_count, own_heads),
        head_first,
        1,
    )
    map_part = jnp.concatenate([d_maps, d_dt_full], axis=1)
    summed = lax.psum(map_part, "dp")
    conv_out, conv_back = jax.vjp(whole_act, pre_part)
    d_pre = conv_back(summed[:, :map_cols])[0]
    round_bcdt = jnp.concatenate([d_pre, summed[:, map_cols:]], axis=1).astype(jnp.bfloat16)
    own_round = (
        jnp.stack(
            [
                d_px.reshape(row_count, own_heads, HEAD_DIM),
                d_pz.reshape(row_count, own_heads, HEAD_DIM),
            ],
            axis=2,
        )
        .reshape(row_count, own_heads * 2 * HEAD_DIM)
        .astype(jnp.bfloat16)
    )
    round_xz = lax.all_gather(own_round, "dp", axis=1, tiled=True)
    grad_xz = transposed_times(normed, round_xz)
    grad_bcdt = transposed_times(round_bcdt, normed)
    d_normed = times_transposed(round_xz, local_xz)
    d_normed = d_normed + jnp.dot(round_bcdt, local_bcdt, preferred_element_type=jnp.float32)
    inner_sum = feature_sum(d_normed * values)[:, None]
    d_norm_in = scales * d_normed - values * (scales * scales * scales) * inner_sum / D
    d_input = (cot_rows.astype(jnp.float32) + d_norm_in).astype(jnp.bfloat16)
    prev_grad = send_along(d_input, -1)
    return (next_act[None], prev_grad[None], grad_xz[None], grad_bcdt[None], grad_out[None])


def solution(mesh):
    return jax.shard_map(
        per_device,
        mesh=mesh,
        in_specs=(
            P("section", None, "dp"),
            P("section", None, "dp"),
            P("section", None, "dp"),
            P("section", "dp", None),
            P("section", None, "dp"),
            P("section", None, "dp"),
            P("section", None, "dp"),
            P("section", None, None),
            P("section", "dp"),
            P("section", "dp"),
            P("section", "dp"),
            P("section", "dp"),
        ),
        out_specs=(
            P("section", None, "dp"),
            P("section", None, "dp"),
            P("section", "dp", None),
            P("section", None, "dp"),
            P("section", None, "dp"),
        ),
        check_vma=False,
    )
```

profile of v0, /device:TPU:0, one launch (start us, length us, event | category | flops | bytes accessed | tf_op | source)
XLA Modules:
  0.0 311.2 jit_solution(6612498661934579519)
XLA Ops:
  7.2 1.1 fusion.86
  8.3 8.4 %psum.66 = f32[128]{0:T(128)S(1)} all-reduce(f32[128]{0:T(128)S(1)} %fusion.86), channel_id=1, replica_groups=mesh['section'=8,'dp'=4] {'dp'}, use_global_device_ids=true, to_apply=%region_8.9 | all-reduce | flops 128 | bytes 1024 | tf_op jit(solution)/shard_map/psum | solution.py:79
  17.2 1.9 fusion.80
  19.2 6.8 %fusion.2 = f32[128,8192]{1,0:T(8,128)} fusion(bf16[1,512,8192]{2,1,0:T(8,128)(2,1)} %param.15, bf16[1,128,512]{2,1,0:T(8,128)(2,1)} %param.13, f32[128]{0:T(128)S(1)} %get-tuple-element.49), kind=kOutput, calls=%fused_computation.3 | convolution fusion | flops 1073938432 | bytes 12714496 | tf_op jit(solution)/shard_map/dot_general | solution.py:129
  26.1 0.8 copy-done.5
  26.9 5.0 %fusion.6 = f32[128,4096]{1,0:T(8,128)} fusion(bf16[1,4096,512]{2,1,0:T(8,128)(2,1)} %param.17, bf16[1,128,512]{2,1,0:T(8,128)(2,1)S(1)} %copy-done.5), kind=kOutput, calls=%fused_computation.8 | convolution fusion | flops 536870912 | bytes 6422528 | tf_op jit(solution)/shard_map/dot_general | solution.py:67
  32.2 19.0 %all-reduce.18.cloned.1.call-done = f32[128,320]{0,1:T(8,128)} async-done(((f32[128,320]{0,1:T(8,128)}), f32[128,320]{0,1:T(8,128)}) %all-reduce.18.cloned.1.call-update) | async-done | bytes 163856 | tf_op jit(solution)/shard_map/psum | solution.py:132
  51.2 0.8 slice.178
  52.4 0.9 slice_bitcast_fusion.3
  53.3 1.9 multiply_convert_fusion.2
  55.4 43.6 %reduce-scatter.6.cloned.1.call-done = f32[128,2048]{1,0:T(8,128)} async-done(((f32[128,8192]{1,0:T(8,128)}), f32[128,2048]{1,0:T(8,128)}) %reduce-scatter.6.cloned.1.call-update) | async-done | bytes 1048592 | tf_op jit(solution)/shard_map/reduce_scatter | solution.py:131
  99.0 1.5 copy.55
  100.6 1.2 fusion.63
  101.8 3.0 multiply_reduce_fusion.3
  104.8 1.2 copy.60
  106.1 27.5 %reduce-scatter.8.cloned.1.call-done = f32[128,1024]{1,0:T(8,128)} async-done(((f32[128,4096]{1,0:T(8,128)}), f32[128,1024]{1,0:T(8,128)}) %reduce-scatter.8.cloned.1.call-update) | async-done | bytes 524304 | tf_op jit(solution)/shard_map/reduce_scatter | solution.py:174
  133.6 1.2 multiply_reduce_fusion.2
  134.7 5.8 %all-reduce.13 = (f32[128]{0:T(128)S(1)}, f32[128]{0:T(128)S(1)}, f32[128]{0:T(128)S(1)}) all-reduce(f32[128]{0:T(128)S(1)} %fusion.84, f32[128]{0:T(128)S(1)} %multiply_reduce_fusion.2, f32[128]{0:T(128)S(1)} %get-tuple-element.20), channel_id=1, replica_groups=mesh['section'=8,'dp'=4] {'dp'}, use_global_device_ids=true, to_apply=%region_1.0 | all-reduce | flops 384 | bytes 3072 | tf_op jit(solution)/shard_map/psum | solution.py:79
  140.5 6.7 %fusion.4 = f32[128,8192]{1,0:T(8,128)} fusion(bf16[1,512,8192]{2,1,0:T(8,128)(2,1)} %param.15, bf16[1,128,512]{2,1,0:T(8,128)(2,1)S(1)} %copy-done.3, f32[128]{0:T(128)S(1)} %add_rsqrt_fusion.3), kind=kOutput, calls=%fused_computation.5 | convolution fusion | flops 1073938432 | bytes 12714496 | tf_op jit(solution)/shard_map/dot_general | solution.py:129
  147.5 2.0 multiply_convert_fusion
  149.7 4.2 %fusion.32 = (f32[16,128]{1,0:T(8,128)S(1)}, f32[16,128]{1,0:T(8,128)S(1)}, f32[16,128]{1,0:T(8,128)}, f32[128,128]{1,0:T(8,128)S(1)}) fusion(f32[16,128]{1,0:T(8,128)S(1)} %get-tuple-element.37, f32[128,128]{1,0:T(8,128)S(1)} %fusion.125, f32[16,128]{1,0:T(8,128)S(1)} %copy.57, pred[128,128]{1,0:T(8,128)(4,1)S(1)} %iota_compare_fusion, ...), kind=kOutput, calls=%fused_computation.47 | convolution fusion | flops 205891584 | bytes 1769472 | tf_op jit(solution)/shard_map/transpose(jvp(bhts,bshp->bthp))/dot_general | solution.py:60
  154.1 1.1 reduce_window_sum.30
  155.7 0.8 fusion.131
  157.2 1.7 fusion.82
  159.1 2.3 fusion.10
  161.7 31.3 %reduce-scatter.4.cloned.1.call-done = f32[128,2048]{1,0:T(8,128)} async-done(((f32[128,8192]{1,0:T(8,128)}), f32[128,2048]{1,0:T(8,128)}) %reduce-scatter.4.cloned.1.call-update) | async-done | bytes 1048592 | tf_op jit(solution)/shard_map/reduce_scatter | solution.py:131
  193.0 1.5 copy.49
  194.6 1.9 broadcast_multiply_fusion.1
  197.0 0.8 copy.63
  198.9 28.8 %all-reduce.20.cloned.1.call-done = (f32[128,320]{0,1:T(8,128)}, f32[128,320]{0,1:T(8,128)}) async-done(((f32[128,320]{0,1:T(8,128)}, f32[128,320]{0,1:T(8,128)}), (f32[128,320]{0,1:T(8,128)}, f32[128,320]{0,1:T(8,128)})) %all-reduce.20.cloned.1.call-update) | async-done | bytes 327696 | tf_op jit(solution)/shard_map/psum | solution.py:132
  227.7 0.9 slice_bitcast_fusion.4
  228.6 0.8 slice.172
  229.4 0.8 slice.312
  230.1 1.0 broadcast_multiply_fusion.4
  231.2 1.2 broadcast_multiply_fusion.5
  233.2 3.3 %multiply_reduce_fusion.4 = (f32[128]{0:T(128)S(1)}, f32[1,128,16,64]{1,3,2,0:T(8,128)S(1)}) fusion(f32[1,128,16,2,64]{1,4,3,2,0:T(8,128)S(1)} %bitcast.276, f32[1,128,16,64]{1,3,2,0:T(8,128)} %bitcast.288, f32[16]{0:T(128)S(1)} %bitcast.320, f32[128,16,64]{0,2,1:T(8,128)} %bitcast.289, f32[16,128]{1,0:T(8,128)S(1)} %get-tuple-element.35, ...), kind=kOutput, calls=%fused_computation.94 | convolution fusion | flops 203816832 | bytes 2204672 | tf_op jit(solution)/shard_map/jvp(bhts,bshp->bthp)/dot_general | solution.py:60
  236.8 15.6 %all-gather.6.cloned.1.call-done = bf16[128,8192]{0,1:T(8,128)(2,1)} async-done(((bf16[128,2048]{0,1:T(8,128)(2,1)}), bf16[128,8192]{0,1:T(8,128)(2,1)}) %all-gather.6.cloned.1.call-update) | async-done | bytes 2097168 | tf_op jit(solution)/shard_map/all_gather | solution.py:206
  252.3 6.9 %fusion = f32[128,512]{1,0:T(8,128)S(1)} fusion(bf16[128,8192]{0,1:T(8,128)(2,1)} %all-gather.6.cloned.1.call-done, bf16[1,512,8192]{2,1,0:T(8,128)(2,1)} %param.15), kind=kOutput, calls=%fused_computation.1 | convolution fusion | flops 1073741824 | bytes 10747904 | tf_op jit(solution)/shard_map/dot_general | solution.py:67
  259.6 6.3 %all-reduce.12 = (f32[128]{0:T(128)S(1)}, f32[128]{0:T(128)S(1)}) all-reduce(f32[128]{0:T(128)S(1)} %get-tuple-element.53, f32[128]{0:T(128)S(1)} %get-tuple-element.55), channel_id=1, replica_groups=mesh['section'=8,'dp'=4] {'dp'}, use_global_device_ids=true, to_apply=%region_6.7 | all-reduce | flops 256 | bytes 2048 | tf_op jit(solution)/shard_map/psum | solution.py:83
  265.9 0.8 multiply_convert_fusion.1
  266.8 1.1 convolution_bitcast_fusion.2
  267.9 3.4 %all-gather.8.cloned.1.call-done = bf16[128,4096]{1,0:T(8,128)(2,1)} async-done(((bf16[128,1024]{1,0:T(8,128)(2,1)}), bf16[128,4096]{1,0:T(8,128)(2,1)}) %all-gather.8.cloned.1.call-update) | async-done | bytes 1048592 | tf_op jit(solution)/shard_map/all_gather | solution.py:173
  271.3 5.9 %convolution_bitcast_fusion.1 = f32[1,4096,512]{2,1,0:T(8,128)} fusion(bf16[128,4096]{1,0:T(8,128)(2,1)} %all-gather.8.cloned.1.call-done, bf16[1,128,512]{2,1,0:T(8,128)(2,1)S(1)} %copy-done.5), kind=kOutput, calls=%fused_computation.7 | convolution fusion | flops 536870912 | bytes 9568256 | tf_op jit(solution)/shard_map/dot_general | solution.py:73
  277.4 4.3 %collective-permute-start.1 = (bf16[128,512]{1,0:T(8,128)(2,1)S(1)}, bf16[128,512]{1,0:T(8,128)(2,1)S(1)}, u32[]{:S(2)}, u32[]{:S(2)}) collective-permute-start(bf16[128,512]{1,0:T(8,128)(2,1)S(1)} %fusion.91), channel_id=1, source_target_pairs={{0,28},{4,0},{8,4},{12,8},{16,12},{20,16},{24,20},{28,24},{1,29},{... | collective-permute-start | bytes 393224 | tf_op jit(solution)/shard_map/ppermute | solution.py:16
  281.7 8.0 %all-gather.4.cloned.1.call-done = bf16[128,4096]{1,0:T(8,128)(2,1)} async-done(((bf16[128,1024]{1,0:T(8,128)(2,1)}), bf16[128,4096]{1,0:T(8,128)(2,1)}) %all-gather.4.cloned.1.call-update) | async-done | bytes 1048592 | tf_op jit(solution)/shard_map/all_gather | solution.py:164
  289.7 3.2 %fusion.17 = bf16[128,512]{1,0:T(8,128)(2,1)S(1)} fusion(bf16[128,4096]{1,0:T(8,128)(2,1)} %all-gather.4.cloned.1.call-done, bf16[1,4096,512]{2,1,0:T(8,128)(2,1)} %param.17, bf16[1,128,512]{2,1,0:T(8,128)(2,1)S(1)} %copy-done.4), kind=kOutput, calls=%fused_computation.28 | convolution fusion | flops 537067520 | bytes 5505024 | tf_op jit(solution)/shard_map/dot_general | solution.py:163
  292.9 1.5 collective-permute-start
  294.4 8.6 %convolution_bitcast_fusion = f32[1,512,8192]{2,1,0:T(8,128)} fusion(bf16[128,8192]{0,1:T(8,128)(2,1)S(1)} %copy-done.1, bf16[1,128,512]{2,1,0:T(8,128)(2,1)S(1)} %copy-done.2, f32[128]{0:T(128)S(1)} %get-tuple-element.49), kind=kOutput, calls=%fused_computation | convolution fusion | flops 1073938432 | bytes 19005952 | tf_op jit(solution)/shard_map/dot_general | solution.py:73
  (115 shorter events, 8.3 us)
Async XLA Ops:
  7.2 10.1 %copy-start = (bf16[1,320,512]{2,1,0:T(8,128)(2,1)S(1)}, bf16[1,320,512]{2,1,0:T(8,128)(2,1)}, u32[]{:S(2)}) copy-start(bf16[1,320,512]{2,1,0:T(8,128)(2,1)} %param.16) | copy-start | bytes 983044
  7.2 44.0 %all-reduce.18.cloned.1.call-start = ((), (), s32[]{:S(2)}) async-start(), calls=%async_computation.6 | async-start | bytes 327680 | tf_op jit(solution)/shard_map/psum | solution.py:132
  19.2 79.8 %reduce-scatter.6.cloned.1.call-start = ((), (), s32[]{:S(2)}) async-start(), calls=%async_computation.5 | async-start | bytes 5242880 | tf_op jit(solution)/shard_map/reduce_scatter | solution.py:131
  26.0 0.9 copy-start.5
  26.0 6.0 %copy-start.3 = (bf16[1,128,512]{2,1,0:T(8,128)(2,1)S(1)}, bf16[1,128,512]{2,1,0:T(8,128)(2,1)}, u32[]{:S(2)}) copy-start(bf16[1,128,512]{2,1,0:T(8,128)(2,1)} %param.12) | copy-start | bytes 393220
  26.0 6.1 %copy-start.26 = (f32[1,16]{1,0:T(1,128)S(1)}, f32[1,16]{1,0:T(1,128)}, u32[]{:S(2)}) copy-start(f32[1,16]{1,0:T(1,128)} %param.21) | copy-start | bytes 196
  26.0 6.1 %copy-start.24 = (f32[1,4,256]{2,1,0:T(4,128)S(1)}, f32[1,4,256]{2,1,0:T(4,128)}, u32[]{:S(2)}) copy-start(f32[1,4,256]{2,1,0:T(4,128)} %param.19) | copy-start | bytes 12292
  26.1 6.1 %copy-start.12 = (f32[1,4,1024]{2,1,0:T(4,128)S(1)}, f32[1,4,1024]{2,1,0:T(4,128)}, u32[]{:S(2)}) copy-start(f32[1,4,1024]{2,1,0:T(4,128)} %param.18) | copy-start | bytes 49156
  26.1 25.9 %copy-start.19 = (f32[1,16]{1,0:T(1,128)S(1)}, f32[1,16]{1,0:T(1,128)}, u32[]{:S(2)}) copy-start(f32[1,16]{1,0:T(1,128)} %param.20) | copy-start | bytes 196
  26.1 107.5 %reduce-scatter.8.cloned.1.call-start = ((), (), s32[]{:S(2)}) async-start(), calls=%async_computation.7 | async-start | bytes 2621440 | tf_op jit(solution)/shard_map/reduce_scatter | solution.py:174
  31.9 69.9 %copy-start.27 = (f32[1,16]{1,0:T(1,128)S(1)}, f32[1,16]{1,0:T(1,128)}, u32[]{:S(2)}) copy-start(f32[1,16]{1,0:T(1,128)} %param.22) | copy-start | bytes 196
  31.9 161.1 %reduce-scatter.4.cloned.1.call-start = ((), (), s32[]{:S(2)}) async-start(), calls=%async_computation.3 | async-start | bytes 5242880 | tf_op jit(solution)/shard_map/reduce_scatter | solution.py:131
  32.1 21.2 %copy-start.21 = (f32[16]{0:T(128)}, f32[16]{0:T(128)S(1)}, u32[]{:S(2)}) copy-start(f32[16]{0:T(128)S(1)} %negate_bitcast_fusion) | copy-start | bytes 196
  32.2 68.4 %copy-start.13 = (f32[1,1,256]{2,1,0:T(1,128)}, f32[1,1,256]{2,1,0:T(1,128)S(1)}, u32[]{:S(2)}) copy-start(f32[1,1,256]{2,1,0:T(1,128)S(1)} %get-tuple-element.44) | copy-start | bytes 3076
  32.2 72.6 %copy-start.15 = (f32[1,1,256]{2,1,0:T(1,128)}, f32[1,1,256]{2,1,0:T(1,128)S(1)}, u32[]{:S(2)}) copy-start(f32[1,1,256]{2,1,0:T(1,128)S(1)} %get-tuple-element.46) | copy-start | bytes 3076
  52.0 97.6 %copy-start.17 = (f32[16,128]{1,0:T(8,128)}, f32[16,128]{1,0:T(8,128)S(1)}, u32[]{:S(2)}) copy-start(f32[16,128]{1,0:T(8,128)S(1)} %get-tuple-element.37) | copy-start | bytes 24580
  52.4 97.3 %copy-start.18 = (f32[16,128]{1,0:T(8,128)}, f32[16,128]{1,0:T(8,128)S(1)}, u32[]{:S(2)}) copy-start(f32[16,128]{1,0:T(8,128)S(1)} %copy.57) | copy-start | bytes 24580
  55.4 94.3 %copy-start.10 = (f32[128,128]{1,0:T(8,128)}, f32[128,128]{1,0:T(8,128)S(1)}, u32[]{:S(2)}) copy-start(f32[128,128]{1,0:T(8,128)S(1)} %fusion.125) | copy-start | bytes 196612
  100.6 33.0 %copy-start.11 = (f32[1,1024]{1,0:T(1,128)S(1)}, f32[1,1024]{1,0:T(1,128)}, u32[]{:S(2)}) copy-start(f32[1,1024]{1,0:T(1,128)} %param.23) | copy-start | bytes 12292
  101.8 45.4 %copy-start.8 = (f32[1,128,1024]{1,2,0:T(8,128)}, f32[1,128,1024]{1,2,0:T(8,128)S(1)}, u32[]{:S(2)}) copy-start(f32[1,128,1024]{1,2,0:T(8,128)S(1)} %get-tuple-element.24) | copy-start | bytes 1572868
  140.5 6.7 %copy-start.23 = (f32[128]{0:T(128)}, f32[128]{0:T(128)S(1)}, u32[]{:S(2)}) copy-start(f32[128]{0:T(128)S(1)} %add_rsqrt_fusion.3) | copy-start | bytes 1540
  147.3 80.4 %all-reduce.20.cloned.1.call-start = ((), (), s32[]{:S(2)}) async-start(), calls=%async_computation.10 | async-start | bytes 655360 | tf_op jit(solution)/shard_map/psum | solution.py:132
  149.7 9.1 %copy-start.7 = (f32[1,128,16,64]{1,3,2,0:T(8,128)S(1)}, f32[1,128,16,64]{1,3,2,0:T(8,128)}, u32[]{:S(2)}) copy-start(f32[1,128,16,64]{1,3,2,0:T(8,128)} %get-tuple-element.52) | copy-start | bytes 1572868
  161.7 90.6 %all-gather.6.cloned.1.call-start = ((), (), s32[]{:S(2)}) async-start(), calls=%async_computation.8 | async-start | bytes 2621440 | tf_op jit(solution)/shard_map/all_gather | solution.py:206
  194.6 35.5 %copy-start.9 = (f32[1,128,256]{1,2,0:T(8,128)S(1)}, f32[1,128,256]{1,2,0:T(8,128)}, u32[]{:S(2)}) copy-start(f32[1,128,256]{1,2,0:T(8,128)} %get-tuple-element.23) | copy-start | bytes 393220
  194.6 36.5 %copy-start.14 = (f32[1,1,256]{2,1,0:T(1,128)S(1)}, f32[1,1,256]{2,1,0:T(1,128)}, u32[]{:S(2)}) copy-start(f32[1,1,256]{2,1,0:T(1,128)} %copy-done.13) | copy-start | bytes 3076
  194.6 36.5 %copy-start.16 = (f32[1,1,256]{2,1,0:T(1,128)S(1)}, f32[1,1,256]{2,1,0:T(1,128)}, u32[]{:S(2)}) copy-start(f32[1,1,256]{2,1,0:T(1,128)} %copy-done.15) | copy-start | bytes 3076
  196.5 36.1 %copy-start.20 = (f32[1,16]{1,0:T(1,128)S(1)}, f32[1,16]{1,0:T(1,128)}, u32[]{:S(2)}) copy-start(f32[1,16]{1,0:T(1,128)} %param.20) | copy-start | bytes 196
  196.5 36.1 %copy-start.22 = (f32[16]{0:T(128)S(1)}, f32[16]{0:T(128)}, u32[]{:S(2)}) copy-start(f32[16]{0:T(128)} %copy-done.21) | copy-start | bytes 196
  196.5 36.7 %copy-start.28 = (f32[1,16]{1,0:T(1,128)S(1)}, f32[1,16]{1,0:T(1,128)}, u32[]{:S(2)}) copy-start(f32[1,16]{1,0:T(1,128)} %param.22) | copy-start | bytes 196
  197.9 73.4 %all-gather.8.cloned.1.call-start = ((), (), s32[]{:S(2)}) async-start(), calls=%async_computation.9 | async-start | bytes 1310720 | tf_op jit(solution)/shard_map/all_gather | solution.py:173
  198.6 91.0 %all-gather.4.cloned.1.call-start = ((), (), s32[]{:S(2)}) async-start(), calls=%async_computation.4 | async-start | bytes 1310720 | tf_op jit(solution)/shard_map/all_gather | solution.py:164
  236.7 22.5 %copy-start.2 = (bf16[1,128,512]{2,1,0:T(8,128)(2,1)S(1)}, bf16[1,128,512]{2,1,0:T(8,128)(2,1)}, u32[]{:S(2)}) copy-start(bf16[1,128,512]{2,1,0:T(8,128)(2,1)} %param.13) | copy-start | bytes 393220
  267.9 9.3 %copy-start.6 = (bf16[1,128,512]{2,1,0:T(8,128)(2,1)S(1)}, bf16[1,128,512]{2,1,0:T(8,128)(2,1)}, u32[]{:S(2)}) copy-start(bf16[1,128,512]{2,1,0:T(8,128)(2,1)} %param.14) | copy-start | bytes 393220
  267.9 9.3 %copy-start.25 = (f32[128]{0:T(128)S(1)}, f32[128]{0:T(128)}, u32[]{:S(2)}) copy-start(f32[128]{0:T(128)} %get-tuple-element.48) | copy-start | bytes 1540
  267.9 21.8 %copy-start.4 = (bf16[1,128,512]{2,1,0:T(8,128)(2,1)S(1)}, bf16[1,128,512]{2,1,0:T(8,128)(2,1)}, u32[]{:S(2)}) copy-start(bf16[1,128,512]{2,1,0:T(8,128)(2,1)} %param.12) | copy-start | bytes 393220
  277.2 17.2 %copy-start.1 = (bf16[128,8192]{0,1:T(8,128)(2,1)S(1)}, bf16[128,8192]{0,1:T(8,128)(2,1)}, u32[]{:S(2)}) copy-start(bf16[128,8192]{0,1:T(8,128)(2,1)} %all-gather.6.cloned.1.call-done) | copy-start | bytes 6291460
  277.4 25.7 %collective-permute-start.1 = (bf16[128,512]{1,0:T(8,128)(2,1)S(1)}, bf16[128,512]{1,0:T(8,128)(2,1)S(1)}, u32[]{:S(2)}, u32[]{:S(2)}) collective-permute-start(bf16[128,512]{1,0:T(8,128)(2,1)S(1)} %fusion.91), channel_id=1, source_target_pairs={{0,28},{4,0},{8,4},{12,8},{16,12},{20,16},{24,20},{28,24},{1,29},{... | collective-permute-start | bytes 393224 | tf_op jit(solution)/shard_map/ppermute | solution.py:16
  292.9 10.1 %collective-permute-start = (bf16[128,512]{1,0:T(8,128)(2,1)S(1)}, bf16[128,512]{1,0:T(8,128)(2,1)S(1)}, u32[]{:S(2)}, u32[]{:S(2)}) collective-permute-start(bf16[128,512]{1,0:T(8,128)(2,1)S(1)} %fusion.17), channel_id=1, source_target_pairs={{0,4},{4,8},{8,12},{12,16},{16,20},{20,24},{24,28},{28,0},{1,5},{5... | collective-permute-start | bytes 393224 | tf_op jit(solution)/shard_map/ppermute | solution.py:16
Sparse Core Ops, SparseCore 0:
  19.3 31.8 all-reduce.17
  54.4 44.5 reduce-scatter.5
  102.1 31.4 reduce-scatter.7
  147.4 45.5 reduce-scatter.3
  195.2 32.4 all-reduce.19
  229.7 22.5 all-gather.5
  254.4 16.8 all-gather.7
  272.9 16.7 all-gather.3
where the time goes:
time: 312 us; the launch traced here: 311 us
  waiting for transfers between devices  178 us (57%)
  matrix products  61.8 us (20%)
  blocking collectives  20.4 us (7%)
  other arithmetic  17.4 us (6%)
  between operations  14.7 us (5%)
  local copies, waits for them, and re-layouts  12.5 us (4%)
  starting transfers between devices  6.58 us (2%)
    reduce_scatter x2, waiting for transfers between devices, project(): own_xz = lax.psum_scatter(part_xz, 'dp', scatter_dimension=1, tiled=True)  74.9 us
    psum x2, waiting for transfers between devices, project(): whole_cols = lax.psum(part_bcdt, 'dp')  47.7 us
    reduce_scatter x1, waiting for transfers between devices, per_device(): lax.psum_scatter(times_transposed(cot_rows, local_out), 'dp', scatter_dim...  27.5 us
    dot_general x3, matrix products, transposed_times(): lax.dot_general(left, right, (((0,), (0,)), ((), ())), preferred_element_...  15.6 us
    all_gather x1, waiting for transfers between devices, per_device(): round_xz = lax.all_gather(own_round, 'dp', axis=1, tiled=True)  15.6 us
    dot_general x4, matrix products, times_transposed(): lax.dot_general(left, right, (((1,), (1,)), ((), ())), preferred_element_...  15.5 us
    psum x2, blocking collectives, feature_sum(): return lax.psum(jnp.sum(values, axis=1), 'dp')  14.1 us
    dot_general x2, matrix products, project(): part_xz = jnp.dot(normed, local_xz, preferred_element_type=jnp.float32)  13.5 us
  transfers between devices with their start and end apart: 10, of which 8 were waited for; matrix products, arithmetic and copies ran while one was open for 25% of the time, Pallas kernels for 0%

commit v1 on v0

--- a/solution.py
+++ b/solution.py
@@ -76,7 +76,7 @@
 
 
 def feature_sum(values):
-    return lax.psum(jnp.sum(values, axis=1), "dp")
+    return jnp.sum(lax.all_gather(jnp.sum(values, axis=1), "dp"), axis=0)
 
 
 def gate_sum(values):

time: 312 us -> 336 us (1.077)
  waiting for transfers between devices: 178 us -> 196 us
    psum x2 -> x1, waiting for transfers between devices: 47.7 us -> 13.5 us  [project(): whole_cols = lax.psum(part_bcdt, 'dp')]
    psum x0 -> x1, waiting for transfers between devices: none -> 27.6 us  [per_device(): summed = lax.psum(map_part, 'dp')]
    all_gather x0 -> x3, blocking collectives: none -> 16.3 us  [feature_sum(): return jnp.sum(lax.all_gather(jnp.sum(values, axis=1), 'dp'), axis=0)]
    psum x2 -> x0, blocking collectives: 14.1 us -> none  [feature_sum(): return lax.psum(jnp.sum(values, axis=1), 'dp')]
    reduce_scatter x2, waiting for transfers between devices: 74.9 us -> 86.4 us  [project(): own_xz = lax.psum_scatter(part_xz, 'dp', scatter_dimension=1, tiled=True)]
    all_gather x1, waiting for transfers between devices: 3.4 us -> 13.9 us  [per_device(): lax.all_gather(mixed_in, 'dp', axis=1, tiled=True)]
    reduce_scatter x1, waiting for transfers between devices: 27.5 us -> 19.5 us  [per_device(): lax.psum_scatter(times_transposed(cot_rows, local_out), 'dp', scatter_dim...]
    all_gather x1, waiting for transfers between devices: 7.98 us -> 14.9 us  [per_device(): lax.all_gather(forward_mixed, 'dp', axis=1, tiled=True)]
  transfers between devices with their start and end apart: 10 -> 10, of which waited for: 8 -> 8; matrix products, arithmetic and copies ran while one was open for 25% -> 20% of each run, Pallas kernels for 0% -> 0%
where the time goes in v1:
time: 336 us; the launch traced here: 335 us
  waiting for transfers between devices  196 us (58%)
  matrix products  64.1 us (19%)
  blocking collectives  22.9 us (7%)
  other arithmetic  16.2 us (5%)
  local copies, waits for them, and re-layouts  14.7 us (4%)
  between operations  14.7 us (4%)
  starting transfers between devices  6.35 us (2%)
    reduce_scatter x2, waiting for transfers between devices, project(): own_xz = lax.psum_scatter(part_xz, 'dp', scatter_dimension=1, tiled=True)  86.4 us
    psum x1, waiting for transfers between devices, per_device(): summed = lax.psum(map_part, 'dp')  27.6 us
    reduce_scatter x1, waiting for transfers between devices, per_device(): lax.psum_scatter(times_transposed(cot_rows, local_out), 'dp', scatter_dim...  19.5 us
    all_gather x1, waiting for transfers between devices, per_device(): round_xz = lax.all_gather(own_round, 'dp', axis=1, tiled=True)  18.9 us
    all_gather x3, blocking collectives, feature_sum(): return jnp.sum(lax.all_gather(jnp.sum(values, axis=1), 'dp'), axis=0)  16.3 us
    dot_general x4, matrix products, times_transposed(): lax.dot_general(left, right, (((1,), (1,)), ((), ())), preferred_element_...  15.9 us
    dot_general x3, matrix products, transposed_times(): lax.dot_general(left, right, (((0,), (0,)), ((), ())), preferred_element_...  15.6 us
    all_gather x1, waiting for transfers between devices, per_device(): lax.all_gather(forward_mixed, 'dp', axis=1, tiled=True)  14.9 us
  transfers between devices with their start and end apart: 10, of which 8 were waited for; matrix products, arithmetic and copies ran while one was open for 20% of the time, Pallas kernels for 0%

profile of v1, /device:TPU:0, one launch (start us, length us, event | category | flops | bytes accessed | tf_op | source)
XLA Modules:
  0.0 334.9 jit_solution(3692360902541815660)
XLA Ops:
  7.2 1.1 fusion.86
  8.3 6.0 %all-gather.4 = f32[4,1,128]{2,1,0:T(1,128)S(1)} all-gather(f32[1,1,128]{2,1,0:T(1,128)S(1)} %bitcast.318), channel_id=3, replica_groups=mesh['section'=8,'dp'=4] {'dp'}, dimensions={0}, use_global_device_ids=true | all-gather | bytes 2560 | tf_op jit(solution)/shard_map/all_gather | solution.py:79
  14.9 1.0 fusion.84
  15.9 5.3 %all-gather.3 = f32[4,1,128]{2,1,0:T(1,128)S(1)} all-gather(f32[1,1,128]{2,1,0:T(1,128)S(1)} %bitcast.319), channel_id=2, replica_groups=mesh['section'=8,'dp'=4] {'dp'}, dimensions={0}, use_global_device_ids=true | all-gather | bytes 2560 | tf_op jit(solution)/shard_map/all_gather | solution.py:79
  21.3 1.9 fusion.82
  23.1 1.9 fusion.80
  25.1 6.8 %fusion.2 = f32[128,8192]{1,0:T(8,128)} fusion(bf16[1,512,8192]{2,1,0:T(8,128)(2,1)} %param.15, bf16[1,128,512]{2,1,0:T(8,128)(2,1)} %param.13, f32[128]{0:T(128)S(1)} %get-tuple-element.50), kind=kOutput, calls=%fused_computation.3 | convolution fusion | flops 1073938432 | bytes 12714496 | tf_op jit(solution)/shard_map/dot_general | solution.py:129
  32.0 0.8 copy-done.3
  32.8 6.7 %fusion.4 = f32[128,8192]{1,0:T(8,128)} fusion(bf16[1,512,8192]{2,1,0:T(8,128)(2,1)} %param.15, bf16[1,128,512]{2,1,0:T(8,128)(2,1)S(1)} %copy-done.3, f32[128]{0:T(128)S(1)} %add_rsqrt_fusion.3), kind=kOutput, calls=%fused_computation.5 | convolution fusion | flops 1073938432 | bytes 12714496 | tf_op jit(solution)/shard_map/dot_general | solution.py:129
  39.6 0.8 copy-done.5
  40.4 5.1 %fusion.6 = f32[128,4096]{1,0:T(8,128)} fusion(bf16[1,4096,512]{2,1,0:T(8,128)(2,1)} %param.17, bf16[1,128,512]{2,1,0:T(8,128)(2,1)S(1)} %copy-done.5), kind=kOutput, calls=%fused_computation.8 | convolution fusion | flops 536870912 | bytes 6422528 | tf_op jit(solution)/shard_map/dot_general | solution.py:67
  45.7 13.5 %all-reduce.19.cloned.1.call-done = (f32[128,320]{0,1:T(8,128)}, f32[128,320]{0,1:T(8,128)}) async-done(((f32[128,320]{0,1:T(8,128)}, f32[128,320]{0,1:T(8,128)}), (f32[128,320]{0,1:T(8,128)}, f32[128,320]{0,1:T(8,128)})) %all-reduce.19.cloned.1.call-update) | async-done | bytes 327696 | tf_op jit(solution)/shard_map/psum | solution.py:132
  59.2 0.8 slice.178
  59.9 0.8 slice.172
  63.3 1.0 slice_bitcast_fusion.3
  64.2 1.4 multiply_convert_fusion.2
  65.8 0.8 fusion.124
  66.7 40.2 %reduce-scatter.6.cloned.1.call-done = f32[128,2048]{1,0:T(8,128)} async-done(((f32[128,8192]{1,0:T(8,128)}), f32[128,2048]{1,0:T(8,128)}) %reduce-scatter.6.cloned.1.call-update) | async-done | bytes 1048592 | tf_op jit(solution)/shard_map/reduce_scatter | solution.py:131
  106.8 1.5 copy.55
  108.4 46.2 %reduce-scatter.4.cloned.1.call-done = f32[128,2048]{1,0:T(8,128)} async-done(((f32[128,8192]{1,0:T(8,128)}), f32[128,2048]{1,0:T(8,128)}) %reduce-scatter.4.cloned.1.call-update) | async-done | bytes 1048592 | tf_op jit(solution)/shard_map/reduce_scatter | solution.py:131
  154.7 1.5 copy.49
  156.3 2.4 fusion.63
  158.6 4.3 %multiply_reduce_fusion.3 = (f32[128]{0:T(128)}, f32[1,128,16,64]{1,3,2,0:T(8,128)}, f32[1,128,16,64]{1,3,2,0:T(8,128)}) fusion(f32[1,128,16,2,64]{1,4,3,2,0:T(8,128)S(1)} %bitcast.274, f32[1,128,16,64]{1,3,2,0:T(8,128)S(1)} %bitcast.287, f32[16]{0:T(128)} %bitcast.320, f32[128,16,64]{0,2,1:T(8,128)S(1)} %bitcast.286, f32[16,128]{1,0:T(8,128)} %get-tuple-element.33, ...), kind=kOutput, calls=%fused_computation.80 | convolution fusion | flops 203816832 | bytes 2728960 | tf_op jit(solution)/shard_map/jvp(bhts,bshp->bthp)/dot_general | solution.py:60
  163.0 1.2 copy.60
  164.2 4.8 %multiply_reduce_fusion.4 = (f32[128]{0:T(128)}, f32[1,128,16,64]{1,3,2,0:T(8,128)}) fusion(f32[1,128,16,2,64]{1,4,3,2,0:T(8,128)S(1)} %bitcast.279, f32[1,128,16,64]{1,3,2,0:T(8,128)} %bitcast.289, f32[16]{0:T(128)} %bitcast.321, f32[128,16,64]{0,2,1:T(8,128)} %bitcast.290, f32[16,128]{1,0:T(8,128)} %get-tuple-element.47, f32[128,128]{1,0:T(8,128)} %fusion.124, ...), kind=kOutput, calls=%fused_computation.94 | convolution fusion | flops 203816832 | bytes 2204672 | tf_op jit(solution)/shard_map/jvp(bhts,bshp->bthp)/dot_general | solution.py:60
  169.0 19.5 %reduce-scatter.8.cloned.1.call-done = f32[128,1024]{1,0:T(8,128)} async-done(((f32[128,4096]{1,0:T(8,128)}), f32[128,1024]{1,0:T(8,128)}) %reduce-scatter.8.cloned.1.call-update) | async-done | bytes 524304 | tf_op jit(solution)/shard_map/reduce_scatter | solution.py:174
  188.5 1.2 multiply_reduce_fusion.2
  189.7 6.6 %all-reduce.12 = (f32[128]{0:T(128)S(1)}, f32[128]{0:T(128)}, f32[128]{0:T(128)S(1)}) all-reduce(f32[128]{0:T(128)} %get-tuple-element.54, f32[128]{0:T(128)S(1)} %multiply_reduce_fusion.2, f32[128]{0:T(128)} %get-tuple-element.18), channel_id=1, replica_groups=mesh['section'=8,'dp'=4] {'dp'}, use_global_device_ids=true, to_apply=%region_6.7 | all-reduce | flops 384 | bytes 3072 | tf_op jit(solution)/shard_map/psum | solution.py:83
  196.8 1.2 copy.54
  198.0 2.1 multiply_convert_fusion
  200.4 3.6 %fusion.32 = (f32[16,128]{1,0:T(8,128)S(1)}, f32[16,128]{1,0:T(8,128)S(1)}, f32[16,128]{1,0:T(8,128)S(1)}, f32[128,128]{1,0:T(8,128)S(1)}) fusion(f32[16,128]{1,0:T(8,128)} %get-tuple-element.33, f32[128,128]{1,0:T(8,128)S(1)} %fusion.125, f32[16,128]{1,0:T(8,128)} %copy.57, pred[128,128]{1,0:T(8,128)(4,1)S(1)} %iota_compare_fusion, ...), kind=kOutput, calls=%fused_computation.47 | convolution fusion | flops 205891584 | bytes 1769472 | tf_op jit(solution)/shard_map/transpose(jvp(bhts,bshp->bthp))/dot_general | solution.py:60
  204.5 1.1 reduce_window_sum.30
  208.0 1.4 fusion.10
  211.0 0.8 copy.63
  211.8 27.6 %all-reduce.17.cloned.1.call-done = f32[128,320]{0,1:T(8,128)} async-done(((f32[128,320]{0,1:T(8,128)}), f32[128,320]{0,1:T(8,128)}) %all-reduce.17.cloned.1.call-update) | async-done | bytes 163856 | tf_op jit(solution)/shard_map/psum | solution.py:191
  239.4 0.8 slice.312
  240.2 1.0 broadcast_multiply_fusion.4
  241.5 1.1 convolution_bitcast_fusion.2
  242.7 14.9 %all-gather.10.cloned.1.call-done = bf16[128,4096]{1,0:T(8,128)(2,1)} async-done(((bf16[128,1024]{1,0:T(8,128)(2,1)}), bf16[128,4096]{1,0:T(8,128)(2,1)}) %all-gather.10.cloned.1.call-update) | async-done | bytes 1048592 | tf_op jit(solution)/shard_map/all_gather | solution.py:164
  257.6 3.2 fusion.17
  260.8 1.7 collective-permute-start
  262.6 13.9 %all-gather.14.cloned.1.call-done = bf16[128,4096]{1,0:T(8,128)(2,1)} async-done(((bf16[128,1024]{1,0:T(8,128)(2,1)}), bf16[128,4096]{1,0:T(8,128)(2,1)}) %all-gather.14.cloned.1.call-update) | async-done | bytes 1048592 | tf_op jit(solution)/shard_map/all_gather | solution.py:173
  276.5 5.9 %convolution_bitcast_fusion.1 = f32[1,4096,512]{2,1,0:T(8,128)} fusion(bf16[128,4096]{1,0:T(8,128)(2,1)} %all-gather.14.cloned.1.call-done, bf16[1,128,512]{2,1,0:T(8,128)(2,1)S(1)} %copy-done.5), kind=kOutput, calls=%fused_computation.7 | convolution fusion | flops 536870912 | bytes 9568256 | tf_op jit(solution)/shard_map/dot_general | solution.py:73
  282.4 18.9 %all-gather.12.cloned.1.call-done = bf16[128,8192]{0,1:T(8,128)(2,1)} async-done(((bf16[128,2048]{0,1:T(8,128)(2,1)}), bf16[128,8192]{0,1:T(8,128)(2,1)}) %all-gather.12.cloned.1.call-update) | async-done | bytes 2097168 | tf_op jit(solution)/shard_map/all_gather | solution.py:206
  301.2 7.1 %fusion = f32[128,512]{1,0:T(8,128)S(1)} fusion(bf16[128,8192]{0,1:T(8,128)(2,1)} %all-gather.12.cloned.1.call-done, bf16[1,512,8192]{2,1,0:T(8,128)(2,1)} %param.15), kind=kOutput, calls=%fused_computation.1 | convolution fusion | flops 1073741824 | bytes 10747904 | tf_op jit(solution)/shard_map/dot_general | solution.py:67
  308.6 5.0 %all-gather.5 = f32[4,1,128]{2,1,0:T(1,128)S(1)} all-gather(f32[1,1,128]{2,1,0:T(1,128)S(1)} %bitcast.317), channel_id=4, replica_groups=mesh['section'=8,'dp'=4] {'dp'}, dimensions={0}, use_global_device_ids=true | all-gather | bytes 2560 | tf_op jit(solution)/shard_map/all_gather | solution.py:79
  313.9 4.3 %collective-permute-start.1 = (bf16[128,512]{1,0:T(8,128)(2,1)S(1)}, bf16[128,512]{1,0:T(8,128)(2,1)S(1)}, u32[]{:S(2)}, u32[]{:S(2)}) collective-permute-start(bf16[128,512]{1,0:T(8,128)(2,1)S(1)} %fusion.91), channel_id=1, source_target_pairs={{0,28},{4,0},{8,4},{12,8},{16,12},{20,16},{24,20},{28,24},{1,29},{... | collective-permute-start | bytes 393224 | tf_op jit(solution)/shard_map/ppermute | solution.py:16
  318.2 8.6 %convolution_bitcast_fusion = f32[1,512,8192]{2,1,0:T(8,128)} fusion(bf16[128,8192]{0,1:T(8,128)(2,1)S(1)} %copy-done.1, bf16[1,128,512]{2,1,0:T(8,128)(2,1)S(1)} %copy-done.2, f32[128]{0:T(128)S(1)} %copy-done.9), kind=kOutput, calls=%fused_computation | convolution fusion | flops 1073938432 | bytes 19005952 | tf_op jit(solution)/shard_map/dot_general | solution.py:73
  (110 shorter events, 11.0 us)
Async XLA Ops:
  7.2 14.1 %copy-start = (bf16[1,320,512]{2,1,0:T(8,128)(2,1)S(1)}, bf16[1,320,512]{2,1,0:T(8,128)(2,1)}, u32[]{:S(2)}) copy-start(bf16[1,320,512]{2,1,0:T(8,128)(2,1)} %param.16) | copy-start | bytes 983044
  7.2 52.0 %all-reduce.19.cloned.1.call-start = ((), (), s32[]{:S(2)}) async-start(), calls=%async_computation.10 | async-start | bytes 655360 | tf_op jit(solution)/shard_map/psum | solution.py:132
  14.9 226.6 %copy-start.8 = (f32[128]{0:T(128)}, f32[128]{0:T(128)S(1)}, u32[]{:S(2)}) copy-start(f32[128]{0:T(128)S(1)} %get-tuple-element.50) | copy-start | bytes 1540
  25.1 81.8 %reduce-scatter.6.cloned.1.call-start = ((), (), s32[]{:S(2)}) async-start(), calls=%async_computation.5 | async-start | bytes 5242880 | tf_op jit(solution)/shard_map/reduce_scatter | solution.py:131
  31.9 0.9 copy-start.3
  31.9 122.7 %reduce-scatter.4.cloned.1.call-start = ((), (), s32[]{:S(2)}) async-start(), calls=%async_computation.3 | async-start | bytes 5242880 | tf_op jit(solution)/shard_map/reduce_scatter | solution.py:131
  39.5 0.9 copy-start.5
  39.5 6.0 %copy-start.24 = (f32[1,16]{1,0:T(1,128)S(1)}, f32[1,16]{1,0:T(1,128)}, u32[]{:S(2)}) copy-start(f32[1,16]{1,0:T(1,128)} %param.21) | copy-start | bytes 196
  39.5 6.0 %copy-start.18 = (f32[1,4,256]{2,1,0:T(4,128)S(1)}, f32[1,4,256]{2,1,0:T(4,128)}, u32[]{:S(2)}) copy-start(f32[1,4,256]{2,1,0:T(4,128)} %param.19) | copy-start | bytes 12292
  39.6 6.1 %copy-start.11 = (f32[1,4,1024]{2,1,0:T(4,128)S(1)}, f32[1,4,1024]{2,1,0:T(4,128)}, u32[]{:S(2)}) copy-start(f32[1,4,1024]{2,1,0:T(4,128)} %param.18) | copy-start | bytes 49156
  39.6 21.1 %copy-start.19 = (f32[1,16]{1,0:T(1,128)S(1)}, f32[1,16]{1,0:T(1,128)}, u32[]{:S(2)}) copy-start(f32[1,16]{1,0:T(1,128)} %param.20) | copy-start | bytes 196
  39.6 148.9 %reduce-scatter.8.cloned.1.call-start = ((), (), s32[]{:S(2)}) async-start(), calls=%async_computation.6 | async-start | bytes 2621440 | tf_op jit(solution)/shard_map/reduce_scatter | solution.py:174
  45.5 193.9 %all-reduce.17.cloned.1.call-start = ((), (), s32[]{:S(2)}) async-start(), calls=%async_computation.8 | async-start | bytes 327680 | tf_op jit(solution)/shard_map/psum | solution.py:191
  45.6 20.0 %copy-start.21 = (f32[16]{0:T(128)}, f32[16]{0:T(128)S(1)}, u32[]{:S(2)}) copy-start(f32[16]{0:T(128)S(1)} %negate_bitcast_fusion) | copy-start | bytes 196
  45.6 20.0 %copy-start.14 = (f32[1,1,256]{2,1,0:T(1,128)}, f32[1,1,256]{2,1,0:T(1,128)S(1)}, u32[]{:S(2)}) copy-start(f32[1,1,256]{2,1,0:T(1,128)S(1)} %get-tuple-element.45) | copy-start | bytes 3076
  45.6 110.6 %copy-start.12 = (f32[1,1,256]{2,1,0:T(1,128)}, f32[1,1,256]{2,1,0:T(1,128)S(1)}, u32[]{:S(2)}) copy-start(f32[1,1,256]{2,1,0:T(1,128)S(1)} %get-tuple-element.46) | copy-start | bytes 3076
  158.6 4.3 %copy-start.7 = (f32[1,128,1024]{1,2,0:T(8,128)}, f32[1,128,1024]{1,2,0:T(8,128)S(1)}, u32[]{:S(2)}) copy-start(f32[1,128,1024]{1,2,0:T(8,128)S(1)} %get-tuple-element.22) | copy-start | bytes 1572868
  163.0 25.5 %copy-start.10 = (f32[1,1024]{1,0:T(1,128)S(1)}, f32[1,1024]{1,0:T(1,128)}, u32[]{:S(2)}) copy-start(f32[1,1024]{1,0:T(1,128)} %param.23) | copy-start | bytes 12292
  200.3 5.4 %copy-start.20 = (f32[1,16]{1,0:T(1,128)S(1)}, f32[1,16]{1,0:T(1,128)}, u32[]{:S(2)}) copy-start(f32[1,16]{1,0:T(1,128)} %param.20) | copy-start | bytes 196
  200.3 5.4 %copy-start.22 = (f32[16]{0:T(128)S(1)}, f32[16]{0:T(128)}, u32[]{:S(2)}) copy-start(f32[16]{0:T(128)} %copy-done.21) | copy-start | bytes 196
  200.3 7.6 %copy-start.16 = (f32[16,128]{1,0:T(8,128)S(1)}, f32[16,128]{1,0:T(8,128)}, u32[]{:S(2)}) copy-start(f32[16,128]{1,0:T(8,128)} %get-tuple-element.33) | copy-start | bytes 24580
  200.4 7.6 %copy-start.17 = (f32[16,128]{1,0:T(8,128)S(1)}, f32[16,128]{1,0:T(8,128)}, u32[]{:S(2)}) copy-start(f32[16,128]{1,0:T(8,128)} %copy.57) | copy-start | bytes 24580
  200.4 7.6 %copy-start.25 = (f32[1,16]{1,0:T(1,128)S(1)}, f32[1,16]{1,0:T(1,128)}, u32[]{:S(2)}) copy-start(f32[1,16]{1,0:T(1,128)} %param.22) | copy-start | bytes 196
  205.9 3.6 %copy-start.4 = (f32[1,128,1024]{1,2,0:T(8,128)S(1)}, f32[1,128,1024]{1,2,0:T(8,128)}, u32[]{:S(2)}) copy-start(f32[1,128,1024]{1,2,0:T(8,128)} %get-tuple-element.23) | copy-start | bytes 1572868
  206.6 51.0 %all-gather.10.cloned.1.call-start = ((), (), s32[]{:S(2)}) async-start(), calls=%async_computation.4 | async-start | bytes 1310720 | tf_op jit(solution)/shard_map/all_gather | solution.py:164
  207.1 69.3 %all-gather.14.cloned.1.call-start = ((), (), s32[]{:S(2)}) async-start(), calls=%async_computation.9 | async-start | bytes 1310720 | tf_op jit(solution)/shard_map/all_gather | solution.py:173
  207.9 93.3 %all-gather.12.cloned.1.call-start = ((), (), s32[]{:S(2)}) async-start(), calls=%async_computation.7 | async-start | bytes 2621440 | tf_op jit(solution)/shard_map/all_gather | solution.py:206
  209.4 1.2 copy-start.6
  209.7 30.5 %copy-start.15 = (f32[1,1,256]{2,1,0:T(1,128)S(1)}, f32[1,1,256]{2,1,0:T(1,128)}, u32[]{:S(2)}) copy-start(f32[1,1,256]{2,1,0:T(1,128)} %copy-done.14) | copy-start | bytes 3076
  210.1 31.0 %copy-start.13 = (f32[1,1,256]{2,1,0:T(1,128)S(1)}, f32[1,1,256]{2,1,0:T(1,128)}, u32[]{:S(2)}) copy-start(f32[1,1,256]{2,1,0:T(1,128)} %copy-done.12) | copy-start | bytes 3076
  210.2 31.4 %copy-start.2 = (bf16[1,128,512]{2,1,0:T(8,128)(2,1)S(1)}, bf16[1,128,512]{2,1,0:T(8,128)(2,1)}, u32[]{:S(2)}) copy-start(bf16[1,128,512]{2,1,0:T(8,128)(2,1)} %param.13) | copy-start | bytes 393220
  260.8 21.6 %collective-permute-start = (bf16[128,512]{1,0:T(8,128)(2,1)S(1)}, bf16[128,512]{1,0:T(8,128)(2,1)S(1)}, u32[]{:S(2)}, u32[]{:S(2)}) collective-permute-start(bf16[128,512]{1,0:T(8,128)(2,1)S(1)} %fusion.17), channel_id=1, source_target_pairs={{0,4},{4,8},{8,12},{12,16},{16,20},{20,24},{24,28},{28,0},{1,5},{5... | collective-permute-start | bytes 393224 | tf_op jit(solution)/shard_map/ppermute | solution.py:16
  282.4 31.3 %copy-start.9 = (f32[128]{0:T(128)S(1)}, f32[128]{0:T(128)}, u32[]{:S(2)}) copy-start(f32[128]{0:T(128)} %copy-done.8) | copy-start | bytes 1540
  282.4 31.3 %copy-start.23 = (f32[128]{0:T(128)S(1)}, f32[128]{0:T(128)}, u32[]{:S(2)}) copy-start(f32[128]{0:T(128)} %get-tuple-element.49) | copy-start | bytes 1540
  301.2 16.9 %copy-start.1 = (bf16[128,8192]{0,1:T(8,128)(2,1)S(1)}, bf16[128,8192]{0,1:T(8,128)(2,1)}, u32[]{:S(2)}) copy-start(bf16[128,8192]{0,1:T(8,128)(2,1)} %all-gather.12.cloned.1.call-done) | copy-start | bytes 6291460
  313.9 12.9 %collective-permute-start.1 = (bf16[128,512]{1,0:T(8,128)(2,1)S(1)}, bf16[128,512]{1,0:T(8,128)(2,1)S(1)}, u32[]{:S(2)}, u32[]{:S(2)}) collective-permute-start(bf16[128,512]{1,0:T(8,128)(2,1)S(1)} %fusion.91), channel_id=1, source_target_pairs={{0,28},{4,0},{8,4},{12,8},{16,12},{20,16},{24,20},{28,24},{1,29},{... | collective-permute-start | bytes 393224 | tf_op jit(solution)/shard_map/ppermute | solution.py:16
Sparse Core Ops, SparseCore 0:
  25.2 33.9 all-reduce.18
  62.3 44.5 reduce-scatter.5
  110.1 44.5 reduce-scatter.3
  157.0 31.4 reduce-scatter.7
  206.7 32.6 all-reduce.16
  240.8 16.7 all-gather.9
  259.7 16.7 all-gather.13
  278.6 22.5 all-gather.11
